TPU v7x, 128 devices: a whole 4x4x4 slice. The times are simulated.
128 devices in a mesh: section: 2 (over core), cin: 8 (over z_hi, y), cout: 8 (over z_lo, x).
Axes of the slice: x: 4, y: 4, z: 4 (z_hi: 2, z_lo: 2; z = z_hi * 2 + z_lo), core: 2. Of those that a mesh axis runs over, the one named last changes fastest.
Arguments:
- inner_features: bfloat16 [2, 784, 2560], P('section', None, ('cin', 'cout')), may hold values from 0 to 2
- block_input: bfloat16 [2, 784, 5120], P('section', None, ('cin', 'cout')), may hold values from -6 to 6
- first_kernel: bfloat16 [9, 2560, 2560], P(None, 'cin', 'cout'), may hold values from -0.0546875 to 0.0546875
- expand_weight: bfloat16 [2560, 5120], P('cout', 'cin'), may hold values from -0.15625 to 0.15625
- reduce_weight: bfloat16 [5120, 5120], P(('cin', 'section'), 'cout'), may hold values from -0.125 to 0.125
- stride_kernel: bfloat16 [9, 5120, 5120], P(None, 'cout', ('section', 'cin')), may hold values from -0.0390625 to 0.0390625
- output_grad: bfloat16 [2, 196, 5120], P(None, None, ('section', 'cin', 'cout')), may hold values from -6 to 6
Outputs:
- inner_gradient: float32 [2, 784, 2560], P('section', None, ('cin', 'cout'))
- input_gradient: bfloat16 [2, 784, 5120], P('section', None, ('cin', 'cout'))
- first_gradient: float32 [9, 2560, 2560], P(None, 'cin', 'cout')
- expand_gradient: float32 [2560, 5120], P('cout', 'cin')
- reduce_gradient: float32 [5120, 5120], P(('cin', 'section'), 'cout')
- stride_gradient: float32 [9, 5120, 5120], P(None, 'cout', ('section', 'cin'))
All inputs are finite; a program needn't handle non-finite values.
Results may differ from a plain program's by a relative error of at most 0.013.
Values may be sent and summed in bfloat16 or wider, within the bound.
A program may use at most 192 MiB of HBM per device.

v0:
```python
import jax
import jax.numpy as jnp
from jax import lax
from jax.sharding import PartitionSpec as P

SIDE = 28


def smooth_gate(values):
    return values * jax.nn.sigmoid(values)


def gate_slope(values):
    logistic = jax.nn.sigmoid(values)
    return logistic * (1.0 + values * (1.0 - logistic))


def flatten_rows(images):
    return images.reshape(images.shape[0] * images.shape[1], images.shape[2])


def project(images, matrix):
    product = jnp.dot(flatten_rows(images), matrix, preferred_element_type=jnp.float32)
    return product.reshape(images.shape[0], images.shape[1], matrix.shape[1])


def project_back(grads, matrix):
    product = lax.dot_general(
        flatten_rows(grads), matrix, (((1,), (1,)), ((), ())), preferred_element_type=jnp.float32
    )
    return product.reshape(grads.shape[0], grads.shape[1], matrix.shape[0])


def outer_rows(left, right):
    return lax.dot_general(
        flatten_rows(left),
        flatten_rows(right),
        (((0,), (0,)), ((), ())),
        preferred_element_type=jnp.float32,
    )


def padded_grid(images, side):
    grid = images.reshape(images.shape[0], side, side, images.shape[2])
    return jnp.pad(grid, ((0, 0), (1, 1), (1, 1), (0, 0)))


def conv_same(images, kernel, side):
    padded = padded_grid(images, side)
    total = jnp.zeros((images.shape[0] * side * side, kernel.shape[2]), jnp.float32)
    for row in range(3):
        for column in range(3):
            window = padded[:, row : row + side, column : column + side, :].reshape(
                -1, images.shape[2]
            )
            total = total + jnp.dot(
                window, kernel[3 * row + column], preferred_element_type=jnp.float32
            )
    return total.reshape(images.shape[0], side * side, kernel.shape[2])


def conv_same_back(grads, kernel, side):
    padded = padded_grid(grads, side)
    total = jnp.zeros((grads.shape[0] * side * side, kernel.shape[1]), jnp.float32)
    for row in range(3):
        for column in range(3):
            window = padded[:, 2 - row : 2 - row + side, 2 - column : 2 - column + side, :].reshape(
                -1, grads.shape[2]
            )
            total = total + lax.dot_general(
                window,
                kernel[3 * row + column],
                (((1,), (1,)), ((), ())),
                preferred_element_type=jnp.float32,
            )
    return total.reshape(grads.shape[0], side * side, kernel.shape[1])


def conv_same_weight(images, grads, side):
    padded = padded_grid(images, side)
    flat = flatten_rows(grads)
    terms = []
    for row in range(3):
        for column in range(3):
            window = padded[:, row : row + side, column : column + side, :].reshape(
                -1, images.shape[2]
            )
            terms.append(
                lax.dot_general(
                    window, flat, (((0,), (0,)), ((), ())), preferred_element_type=jnp.float32
                )
            )
    return jnp.stack(terms)


def conv_half_back(grads, kernel, side):
    half = side // 2
    count = grads.shape[0]
    flat = flatten_rows(grads)
    canvas = None
    for row in range(3):
        for column in range(3):
            term = lax.dot_general(
                flat,
                kernel[3 * row + column],
                (((1,), (1,)), ((), ())),
                preferred_element_type=jnp.float32,
            )
            term = term.reshape(count, half, half, kernel.shape[1])
            placed = lax.pad(
                term,
                jnp.zeros((), term.dtype),
                ((0, 0, 0), (row, 3 - row, 1), (column, 3 - column, 1), (0, 0, 0)),
            )
            canvas = placed if canvas is None else canvas + placed
    return canvas[:, 1 : side + 1, 1 : side + 1, :].reshape(count, side * side, kernel.shape[1])


def conv_half_weight(images, grads, side):
    padded = padded_grid(images, side)
    flat = flatten_rows(grads)
    terms = []
    for row in range(3):
        for column in range(3):
            window = padded[:, row : row + side : 2, column : column + side : 2, :].reshape(
                -1, images.shape[2]
            )
            terms.append(
                lax.dot_general(
                    window, flat, (((0,), (0,)), ((), ())), preferred_element_type=jnp.float32
                )
            )
    return jnp.stack(terms)


def gather_outer(shard):
    return lax.all_gather(shard, "cout", axis=2, tiled=True)


def gather_inner(shard):
    return lax.all_gather(shard, "cin", axis=2, tiled=True)


def sum_inner(partial_value):
    return lax.psum_scatter(partial_value, "cin", scatter_dimension=2, tiled=True)


def sum_outer(partial_value):
    return lax.psum_scatter(partial_value, "cout", scatter_dimension=2, tiled=True)


def shards(
    inner_features,
    block_input,
    first_kernel,
    expand_weight,
    reduce_weight,
    stride_kernel,
    output_grad,
):
    feature_block = gather_outer(inner_features)
    first_hidden = sum_inner(conv_same(feature_block, first_kernel, SIDE))
    first_act = smooth_gate(first_hidden).astype(jnp.bfloat16)
    first_block = gather_inner(first_act)
    expanded = sum_outer(project(first_block, expand_weight))
    joined_pre = block_input.astype(jnp.float32) + expanded
    joined = smooth_gate(joined_pre).astype(jnp.bfloat16)
    joined_wide = gather_outer(joined)
    joined_pair = lax.all_to_all(joined_wide, "section", split_axis=2, concat_axis=0, tiled=True)
    hidden_part = project(joined_pair, reduce_weight)
    cotangent_block = gather_outer(output_grad)
    back_part = conv_half_back(cotangent_block, stride_kernel, SIDE)
    hidden_whole = lax.psum(hidden_part, ("section", "cin"))
    second_act = smooth_gate(hidden_whole).astype(jnp.bfloat16)
    back_whole = lax.psum(back_part, ("section", "cin"))
    masked_second = (back_whole * gate_slope(hidden_whole)).astype(jnp.bfloat16)
    stride_gradient = conv_half_weight(second_act, cotangent_block, SIDE)
    reduce_gradient = outer_rows(joined_pair, masked_second)
    joined_back = project_back(masked_second, reduce_weight)
    joined_home = lax.all_to_all(joined_back, "section", split_axis=0, concat_axis=2, tiled=True)
    back_joined = sum_outer(joined_home)
    input_gradient = (back_joined * gate_slope(joined_pre)).astype(jnp.bfloat16)
    input_wide = gather_outer(input_gradient)
    expand_local = outer_rows(first_block, input_wide)
    back_first = sum_inner(project_back(input_wide, expand_weight))
    masked_first = (back_first * gate_slope(first_hidden)).astype(jnp.bfloat16)
    masked_block = gather_inner(masked_first)
    inner_gradient = sum_outer(conv_same_back(masked_block, first_kernel, SIDE))
    first_local = conv_same_weight(feature_block, masked_block, SIDE)
    first_gradient, expand_gradient = (
        lax.psum(first_local.astype(jnp.bfloat16), "section").astype(jnp.float32),
        lax.psum(expand_local.astype(jnp.bfloat16), "section").astype(jnp.float32),
    )
    return (
        inner_gradient,
        input_gradient,
        first_gradient,
        expand_gradient,
        reduce_gradient,
        stride_gradient,
    )


def solution(mesh):
    return jax.shard_map(
        shards,
        mesh=mesh,
        in_specs=(
            P("section", None, ("cin", "cout")),
            P("section", None, ("cin", "cout")),
            P(None, "cin", "cout"),
            P("cout", "cin"),
            P(("cin", "section"), "cout"),
            P(None, "cout", ("section", "cin")),
            P(None, None, ("section", "cin", "cout")),
        ),
        out_specs=(
            P("section", None, ("cin", "cout")),
            P("section", None, ("cin", "cout")),
            P(None, "cin", "cout"),
            P("cout", "cin"),
            P(("cin", "section"), "cout"),
            P(None, "cout", ("section", "cin")),
        ),
        check_vma=False,
    )
```

profile of v0, /device:TPU:0, one launch (start us, length us, event | category | flops | bytes accessed | tf_op | source)
XLA Modules:
  0.0 957.9 jit_solution(9622084547646178098)
XLA Ops:
  7.2 30.3 %all_gather.19 = bf16[1,784,320]{1,2,0:T(8,128)(2,1)S(1)} all-gather(bf16[1,784,40]{1,2,0:T(8,128)(2,1)} %param.7), channel_id=1, replica_groups=mesh['section'=2,'cin'=8,'cout'=8] {'cout'}, dimensions={2}, use_global_device_ids=true | all-gather | bytes 564480 | tf_op jit(solution)/shard_map/all_gather | solution.py:137
  68.5 28.8 %all_gather.18 = bf16[2,196,320]{1,2,0:T(8,128)(2,1)S(1)} all-gather(bf16[2,196,40]{1,2,0:T(8,128)(2,1)S(1)} %copy-done.55), channel_id=1, replica_groups=mesh['section'=2,'cin'=8,'cout'=8] {'cout'}, dimensions={2}, use_global_device_ids=true | all-gather | bytes 282240 | tf_op jit(solution)/shard_map/all_gather | solution.py:137
  102.0 16.4 %pad.56 = f32[2,28,28,640]{3,2,1,0:T(8,128)} pad(f32[2,14,14,640]{3,2,1,0:T(8,128)} %fusion.54, f32[]{:T(128)} %constant.3.clone.1), padding=0_0_0x1_0_1x1_0_1x0_0_0 | pad | bytes 5017604 | tf_op jit(solution)/shard_map/slice | solution.py:116
  118.4 11.1 %pad.55 = f32[2,28,28,640]{3,2,1,0:T(8,128)} pad(f32[2,14,14,640]{3,2,1,0:T(8,128)S(1)} %fusion.56, f32[]{:T(128)} %constant.3.clone.1), padding=0_0_0x1_0_1x0_1_1x0_0_0 | pad | bytes 5017604 | tf_op jit(solution)/shard_map/slice | solution.py:116
  131.0 11.1 %pad.53 = f32[2,28,28,640]{3,2,1,0:T(8,128)} pad(f32[2,14,14,640]{3,2,1,0:T(8,128)S(1)} %fusion.60, f32[]{:T(128)} %constant.3.clone.1), padding=0_0_0x0_1_1x1_0_1x0_0_0 | pad | bytes 5017604 | tf_op jit(solution)/shard_map/slice | solution.py:116
  143.6 11.1 %pad.52 = f32[2,28,28,640]{3,2,1,0:T(8,128)} pad(f32[2,14,14,640]{3,2,1,0:T(8,128)S(1)} %fusion.62, f32[]{:T(128)} %constant.3.clone.1), padding=0_0_0x0_1_1x0_1_1x0_0_0 | pad | bytes 5017604 | tf_op jit(solution)/shard_map/slice | solution.py:116
  156.2 11.3 %pad.41 = f32[2,30,30,640]{3,2,1,0:T(8,128)} pad(f32[2,14,14,640]{3,2,1,0:T(8,128)S(1)} %fusion.66, f32[]{:T(128)} %constant.3.clone.1), padding=0_0_0x0_3_1x2_1_1x0_0_0 | pad | bytes 5611524 | tf_op jit(solution)/shard_map/pad | solution.py:110
  168.9 11.2 %pad.39 = f32[2,30,30,640]{3,2,1,0:T(8,128)} pad(f32[2,14,14,640]{3,2,1,0:T(8,128)S(1)} %fusion.70, f32[]{:T(128)} %constant.3.clone.1), padding=0_0_0x0_3_1x0_3_1x0_0_0 | pad | bytes 5611524 | tf_op jit(solution)/shard_map/pad | solution.py:110
  181.6 11.3 %pad.40 = f32[2,30,30,640]{3,2,1,0:T(8,128)} pad(f32[2,14,14,640]{3,2,1,0:T(8,128)S(1)} %fusion.68, f32[]{:T(128)} %constant.3.clone.1), padding=0_0_0x0_3_1x1_2_1x0_0_0 | pad | bytes 5611524 | tf_op jit(solution)/shard_map/pad | solution.py:110
  194.4 11.1 %pad.74 = f32[2,28,29,640]{3,2,1,0:T(8,128)} pad(f32[2,14,14,640]{3,2,1,0:T(8,128)S(1)} %fusion.64, f32[]{:T(128)} %constant.3.clone.1), padding=0_0_0x0_1_1x0_2_1x0_0_0 | pad | bytes 5160964
  207.0 11.2 %pad.73 = f32[2,28,29,640]{3,2,1,0:T(8,128)} pad(f32[2,14,14,640]{3,2,1,0:T(8,128)S(1)} %fusion.58, f32[]{:T(128)} %constant.3.clone.1), padding=0_0_0x1_0_1x0_2_1x0_0_0 | pad | bytes 5160964
  219.1 36.6 %all_gather.20 = bf16[1,784,320]{1,2,0:T(8,128)(2,1)S(1)} all-gather(bf16[1,784,40]{1,2,0:T(8,128)(2,1)S(1)} %multiply_convert_fusion.4), channel_id=1, replica_groups=mesh['section'=2,'cin'=8,'cout'=8] {'cin'}, dimensions={2}, use_global_device_ids=true | all-gather | bytes 564480 | tf_op jit(solution)/shard_map/all_gather | solution.py:141
  261.8 6.8 add_add_fusion
  268.6 11.1 %fusion.4 = f32[2,28,28,640]{3,2,1,0:T(8,128)S(1)} fusion(f32[2,28,28,640]{3,2,1,0:T(8,128)} %pad.56, f32[2,28,28,640]{3,2,1,0:T(8,128)} %pad.55, f32[2,28,28,640]{3,2,1,0:T(8,128)} %pad.53, f32[2,28,28,640]{3,2,1,0:T(8,128)} %pad.52, f32[2,30,30,640]{3,2,1,0:T(8,128)S(1)} %add_add_fusion, f32[2,28,29,640]{3,2,1,0:T(8,128)} %pad.74, f32[2,28,29,640]{3,2,1,0:T(8,128)} %pad.73), kind=kLoop, calls=%fused_computation.6 | loop fusion | flops 6021120 | bytes 32112640 | tf_op jit(solution)/shard_map/add | solution.py:115
  286.3 58.8 %all-reduce.24.cloned.1.call-done = f32[1,784,640]{1,0,2:T(1,128)} async-done(((f32[1,784,640]{1,0,2:T(1,128)}), f32[1,784,640]{1,0,2:T(1,128)}) %all-reduce.24.cloned.1.call-update) | async-done | bytes 2007056
  346.9 31.0 %all_gather.21 = bf16[1,784,640]{1,2,0:T(8,128)(2,1)S(1)} all-gather(bf16[1,784,80]{1,2,0:T(8,128)(2,1)S(1)} %multiply_convert_fusion.2), channel_id=1, replica_groups=mesh['section'=2,'cin'=8,'cout'=8] {'cout'}, dimensions={2}, use_global_device_ids=true | all-gather | bytes 1128960 | tf_op jit(solution)/shard_map/all_gather | solution.py:137
  380.2 9.0 reduce
  404.7 195.4 %all-reduce.28.cloned.1.call-done = (f32[2,784,640]{2,1,0:T(8,128)}, f32[2,784,640]{2,1,0:T(8,128)}) async-done(((f32[2,784,640]{2,1,0:T(8,128)}, f32[2,784,640]{2,1,0:T(8,128)}), (f32[2,784,640]{2,1,0:T(8,128)}, f32[2,784,640]{2,1,0:T(8,128)})) %all-reduce.28.cloned.1.call-update) | async-done | bytes 8028176 | tf_op jit(solution)/shard_map/psum | solution.py:175
  616.0 83.4 %all-reduce.26.cloned.1.call-done = f32[1,784,640]{1,0,2:T(1,128)} async-done(((f32[1,784,640]{1,0,2:T(1,128)}), f32[1,784,640]{1,0,2:T(1,128)}) %all-reduce.26.cloned.1.call-update) | async-done | bytes 2007056
  700.6 30.6 %all_gather.22 = bf16[1,784,640]{1,2,0:T(8,128)(2,1)S(1)} all-gather(bf16[1,784,80]{1,2,0:T(8,128)(2,1)S(1)} %fusion.85), channel_id=1, replica_groups=mesh['section'=2,'cin'=8,'cout'=8] {'cout'}, dimensions={2}, use_global_device_ids=true | all-gather | bytes 1128960 | tf_op jit(solution)/shard_map/all_gather | solution.py:137
  756.3 45.9 %reduce-scatter.16.cloned.1.call-done = f32[1,784,40]{1,2,0:T(8,128)} async-done(((f32[1,784,320]{1,2,0:T(8,128)}), f32[1,784,40]{1,2,0:T(8,128)}) %reduce-scatter.16.cloned.1.call-update) | async-done | bytes 125456
  803.2 35.5 %all_gather.23 = bf16[1,784,320]{1,2,0:T(8,128)(2,1)S(1)} all-gather(bf16[1,784,40]{1,2,0:T(8,128)(2,1)S(1)} %multiply_convert_fusion.3), channel_id=1, replica_groups=mesh['section'=2,'cin'=8,'cout'=8] {'cin'}, dimensions={2}, use_global_device_ids=true | all-gather | bytes 564480 | tf_op jit(solution)/shard_map/all_gather | solution.py:141
  841.3 6.5 pad_slice_fusion.4
  911.7 38.9 %reduce-scatter.18.cloned.1.call-done = f32[1,784,40]{1,2,0:T(8,128)} async-done(((f32[1,784,320]{1,2,0:T(8,128)}), f32[1,784,40]{1,2,0:T(8,128)}) %reduce-scatter.18.cloned.1.call-update) | async-done | bytes 125456
  (248 shorter events, 187.6 us)
Async XLA Ops:
  7.2 394.1 %copy-start = (bf16[320,640]{1,0:T(8,128)(2,1)S(1)}, bf16[320,640]{1,0:T(8,128)(2,1)}, u32[]{:S(2)}) copy-start(bf16[320,640]{1,0:T(8,128)(2,1)} %param.11) | copy-start | bytes 1228804
  7.2 211.0 %reduce-scatter.14.cloned.1.call-start = ((), (), s32[]{:S(2)}) async-start(), calls=%async_computation.7 | async-start | bytes 1290240
  42.1 6.6 copy-start.1
  68.4 276.6 %all-reduce.24.cloned.1.call-start = ((), (), s32[]{:S(2)}) async-start(), calls=%async_computation.5 | async-start | bytes 4587520
  206.9 49.6 %copy-start.48 = (bf16[320,640]{1,0:T(8,128)(2,1)S(1)}, bf16[320,640]{1,0:T(8,128)(2,1)}, u32[]{:S(2)}) copy-start(bf16[320,640]{1,0:T(8,128)(2,1)} %param.10) | copy-start | bytes 1228804
  261.5 338.7 %all-reduce.28.cloned.1.call-start = ((), (), s32[]{:S(2)}) async-start(), calls=%async_computation.10 | async-start | bytes 16056320 | tf_op jit(solution)/shard_map/psum | solution.py:175
  282.8 63.3 %copy-start.52 = (bf16[1,784,80]{1,2,0:T(8,128)(2,1)S(1)}, bf16[1,784,80]{1,2,0:T(8,128)(2,1)}, u32[]{:S(2)}) copy-start(bf16[1,784,80]{1,2,0:T(8,128)(2,1)} %param.8) | copy-start | bytes 376324
  404.7 294.7 %all-reduce.26.cloned.1.call-start = ((), (), s32[]{:S(2)}) async-start(), calls=%async_computation.6 | async-start | bytes 4587520
  615.9 84.6 %copy-start.15 = (f32[1,784,80]{1,0,2:T(1,128)S(1)}, f32[1,784,80]{1,0,2:T(1,128)}, u32[]{:S(2)}) copy-start(f32[1,784,80]{1,0,2:T(1,128)} %copy-done.14) | copy-start | bytes 752644
  615.9 116.3 %copy-start.49 = (bf16[320,640]{1,0:T(8,128)(2,1)S(1)}, bf16[320,640]{1,0:T(8,128)(2,1)}, u32[]{:S(2)}) copy-start(bf16[320,640]{1,0:T(8,128)(2,1)} %param.10) | copy-start | bytes 1228804
  615.9 186.3 %reduce-scatter.16.cloned.1.call-start = ((), (), s32[]{:S(2)}) async-start(), calls=%async_computation.8 | async-start | bytes 1290240
  700.6 33.3 %copy-start.51 = (bf16[1,784,80]{1,2,0:T(8,128)(2,1)}, bf16[1,784,80]{1,2,0:T(8,128)(2,1)S(1)}, u32[]{:S(2)}) copy-start(bf16[1,784,80]{1,2,0:T(8,128)(2,1)S(1)} %fusion.85) | copy-start | bytes 376324
  733.9 172.8 %all-reduce.30.cloned.1.call-start = ((), (), s32[]{:S(2)}) async-start(), calls=%async_computation.11 | async-start | bytes 5242880 | tf_op jit(solution)/shard_map/psum | solution.py:191
  748.9 5.8 copy-start.10
  749.9 4.9 copy-start.36
  752.3 49.9 %copy-start.53 = (f32[1,784,40]{1,2,0:T(8,128)S(1)}, f32[1,784,40]{1,2,0:T(8,128)}, u32[]{:S(2)}) copy-start(f32[1,784,40]{1,2,0:T(8,128)} %reduce-scatter.14.cloned.1.call-done) | copy-start | bytes 376324
  754.8 84.3 %copy-start.27 = (bf16[784,320]{1,0:T(8,128)(2,1)S(1)}, bf16[784,320]{1,0:T(8,128)(2,1)}, u32[]{:S(2)}) copy-start(bf16[784,320]{1,0:T(8,128)(2,1)} %reshape.186) | copy-start | bytes 1505284
  841.3 8.6 copy-start.2
  867.7 5.2 copy-start.7
  867.7 5.2 copy-start.17
  870.3 5.0 copy-start.26
  880.4 70.2 %reduce-scatter.18.cloned.1.call-start = ((), (), s32[]{:S(2)}) async-start(), calls=%async_computation.9 | async-start | bytes 1290240
  895.6 4.1 copy-start.46
  906.7 4.1 copy-start.54
  (40 other events, 77.3 us)
Sparse Core Ops, SparseCore 0:
  68.6 69.3 reduce-scatter.13
  261.6 83.4 all-reduce.23
  404.8 195.3 all-reduce.27
  616.1 83.3 all-reduce.25
  734.0 68.1 reduce-scatter.15
  880.6 26.0 all-reduce.29
  909.6 40.9 reduce-scatter.17
where the time goes:
time: 967 us; the launch traced here: 958 us
  waiting for transfers between devices  425 us (44%)
  local copies, waits for them, and re-layouts  203 us (21%)
  blocking collectives  203 us (21%)
  matrix products  70.4 us (7%)
  other arithmetic  39.2 us (4%)
  between operations  15.9 us (2%)
    unnamed x12, waiting for transfers between devices  227 us
    psum x1, waiting for transfers between devices, shards(): back_whole = lax.psum(back_part, ('section', 'cin'))  195 us
    all_gather x4, blocking collectives, gather_outer(): return lax.all_gather(shard, 'cout', axis=2, tiled=True)  121 us
    all_gather x2, blocking collectives, gather_inner(): return lax.all_gather(shard, 'cin', axis=2, tiled=True)  72.1 us
    slice x5, local copies, waits for them, and re-layouts, conv_half_back(): canvas[:, 1:side + 1, 1:side + 1, :]  52.9 us
    unnamed x123, local copies, waits for them, and re-layouts  39.9 us
    pad x3, local copies, waits for them, and re-layouts, conv_half_back(): lax.pad(term, jnp.zeros((), term.dtype), ((0, 0, 0), (row, 3 - row, 1), (...  33.8 us
  transfers between devices with their start and end apart: 7, of which 6 were waited for; matrix products, arithmetic and copies ran while one was open for 20% of the time, Pallas kernels for 0%

commit v1 on v0

v1 whole, which is shorter than its diff:
```python
import functools

import jax
import jax.numpy as jnp
import numpy as np
from jax import lax
from jax.experimental import pallas as pl
from jax.experimental.pallas import tpu as pltpu
from jax.sharding import PartitionSpec as P

MESH = pl.DeviceIdType.MESH
BF = jnp.bfloat16
F32 = jnp.float32

SIDE = 28
HALF = 14
PIX = 896
PLANE = 224
LANES = 128
TALL = 48
CHUNKS = 7
HALVES = ((0, 512), (512, 384))


def sigmoid(v):
    return 1.0 / (1.0 + jnp.exp(-v))


def gate(v):
    return v * sigmoid(v)


def slope(v):
    s = sigmoid(v)
    return s * (1.0 + v * (1.0 - s))


def parity_index():
    y, x = np.divmod(np.arange(SIDE * SIDE), SIDE)
    return ((y % 2) * 2 + x % 2) * PLANE + (y // 2) * 16 + x // 2


def natural_index():
    y, x = np.divmod(np.arange(SIDE * SIDE), SIDE)
    return y * 32 + x


def one_hot(rows, columns, shape):
    out = np.zeros(shape, np.float32)
    out[rows, columns] = 1.0
    return out


def place_natural():
    return one_hot(np.arange(SIDE * SIDE), natural_index(), (SIDE * SIDE, PIX))


def place_parity():
    return one_hot(np.arange(SIDE * SIDE), parity_index(), (SIDE * SIDE, PIX))


def natural_to_parity():
    return one_hot(natural_index(), parity_index(), (PIX, PIX))


def place_grad():
    a, b = np.divmod(np.arange(HALF * HALF), HALF)
    return one_hot(np.arange(HALF * HALF), a * 16 + b, (HALF * HALF, 256))


RANGES = ((0, 256), (128, 384), (384, 384), (640, 256))
PLANE_TAPS = (
    ((4, 0, 0),),
    ((5, 0, 0), (3, 0, 1)),
    ((7, 0, 0), (1, 1, 0)),
    ((8, 0, 0), (6, 0, 1), (2, 1, 0), (0, 1, 1)),
)


def tap_table():
    table, at = [], 0
    for plane, taps in enumerate(PLANE_TAPS):
        for tap, _, _ in taps:
            table.append((plane, tap, at))
            at += RANGES[plane][1]
    return table, at


TAPS, PLACED = tap_table()


def spread_grad():
    out = np.zeros((256, PLACED), np.float32)
    entry = 0
    for plane, taps in enumerate(PLANE_TAPS):
        for _, sy, sx in taps:
            at = TAPS[entry][2] + plane * PLANE - RANGES[plane][0]
            entry += 1
            for a in range(HALF - sy):
                for b in range(HALF - sx):
                    out[(a + sy) * 16 + b + sx, at + a * 16 + b] = 1.0
    return out


def signal(devices):
    barrier = pltpu.get_barrier_semaphore()
    for device in devices:
        pl.semaphore_signal(barrier, inc=1, device_id=device, device_id_type=MESH)
    return lambda: pl.semaphore_wait(barrier, len(devices))


def started(src, dst, sem):
    copy = pltpu.make_async_copy(src, dst, sem)
    copy.start()
    return copy


def remote(src, dst, send, recv, device):
    return pltpu.make_async_remote_copy(
        src_ref=src, dst_ref=dst, send_sem=send, recv_sem=recv, device_id=device, device_id_type=MESH
    )


def rows_at(block, size):
    return pl.ds(pl.multiple_of(block * size, size), size)


def others(axis, size=8):
    me = lax.axis_index(axis)
    return [lax.rem(me + d, size) for d in range(1, size)]


def call(body, outs, scratch, collective_id, *args, far_in=(), far_out=()):
    near, far = pl.BlockSpec(memory_space=pltpu.VMEM), pl.BlockSpec(memory_space=pl.ANY)
    return pl.pallas_call(
        body,
        out_shape=tuple(jax.ShapeDtypeStruct(s, d) for s, d in outs),
        in_specs=[far if n in far_in else near for n in range(len(args))],
        out_specs=tuple(far if n in far_out else near for n in range(len(outs))),
        scratch_shapes=scratch,
        compiler_params=pltpu.CompilerParams(
            collective_id=collective_id, has_side_effects=True, vmem_limit_bytes=56 * 2**20
        ),
    )(*args)


def dot(left, right, contract, kind=F32):
    return lax.dot_general(left, right, (contract, ((), ())), preferred_element_type=F32).astype(kind)


NN = ((1,), (0,))
TN = ((0,), (0,))
NT = ((1,), (1,))


def patches_of(x_ref, out_ref, wide):
    size = x_ref.shape[0]
    lane = lax.broadcasted_iota(jnp.int32, (1, PIX), 1)
    for tx in range(3):
        dx = tx - 1
        wide[...] = pltpu.roll(x_ref[...], (PIX - dx) % PIX, 1) if dx else x_ref[...]
        for ty in range(3):
            dy = ty - 1
            at = (3 * ty + tx) * size
            if dy:
                moved = pltpu.roll(wide[...], (PIX - 32 * dy) % PIX, 1)
                keep = (lane + 32 * dy >= 0) & (lane + 32 * dy < PIX)
                out_ref[at : at + size, :] = jnp.where(keep, moved, 0.0).astype(BF)
            else:
                out_ref[at : at + size, :] = wide[...].astype(BF)


def gather_phase(
    met, feature_ref, grads_ref, natural_ref, spot_ref, patches_ref, patches_save, grad_ref, own, grads_own, gathered,
    grads_gathered, grid, wide, send, recv,
):
    me = lax.axis_index("cout")
    narrow, size = feature_ref.shape[0], own.shape[0]
    own[...] = jnp.concatenate(
        [dot(feature_ref[...], natural_ref[...], NN), jnp.zeros((size - narrow, PIX), F32)], axis=0
    ).astype(BF)
    placed = [dot(grads_ref[image], spot_ref[...], NN) for image in range(2)]
    grads_own[...] = jnp.concatenate(
        [jnp.concatenate(placed, axis=1), jnp.zeros((size - narrow, 512), F32)], axis=0
    ).astype(BF)
    met()
    copies = []
    for n, (source, target) in enumerate(((own, gathered), (grads_own, grads_gathered))):
        for d, peer in enumerate(others("cout")):
            copy = remote(
                source, target.at[rows_at(me, size)], send.at[7 * n + d], recv.at[7 * n + d], {"cout": peer}
            )
            copy.start()
            copies.append(copy)
        target[rows_at(me, size), :] = source[...]
    for copy in copies[:7]:
        copy.wait_recv()
    for j in range(8):
        grid[j * narrow : (j + 1) * narrow, :] = gathered[j * size : (j + 1) * size, :].astype(F32)[:narrow]
    patches_of(grid, patches_ref, wide)
    patches_save.start()

    def cotangent():
        for copy in copies[7:]:
            copy.wait_recv()
        for j in range(8):
            block = grads_gathered[j * size : (j + 1) * size, :].astype(F32)
            wide[j * narrow : (j + 1) * narrow, :512] = block[:narrow]
        for image in range(2):
            grad_ref[image] = wide[:, image * 256 : (image + 1) * 256].astype(BF)
        for copy in copies:
            copy.wait_send()

    return cotangent


def inner_exchange(met, prepare, part_of, finish, fill, out_ref, sbuf, rbuf, sems):
    send, recv, send2, recv2 = sems
    me = lax.axis_index("cin")
    peers = others("cin")
    rows = [slice(0, LANES), slice(LANES, out_ref.shape[0])]
    spot = lax.rem(me, CHUNKS)
    first, second = {}, {}
    for h in range(2):
        prepare(rows[h])
        if h == 0:
            met()
        for d, peer in enumerate(peers):
            n = 7 * h + d
            first[h, d] = remote(
                sbuf.at[peer, rows[h]], rbuf.at[d, rows[h]], send.at[n], recv.at[n], {"cin": peer}
            )
            second[h, d] = remote(
                sbuf.at[7, rows[h]], out_ref.at[rows[h], rows_at(spot, LANES)], send2.at[n], recv2.at[n], {"cin": peer}
            )

            @pl.when(peer < CHUNKS)
            def _(h=h, d=d, peer=peer):
                sbuf[peer, rows[h]] = part_of(peer, rows[h]).astype(BF)
                first[h, d].start()

    fill(0)

    @pl.when(me < CHUNKS)
    def _():
        for h in range(2):
            total = part_of(me, rows[h])
            for d in range(7):
                first[h, d].wait_recv()
                total = total + rbuf[d, rows[h]].astype(F32)
            result = finish(total, rows[h])
            sbuf[7, rows[h]] = result
            for d in range(7):
                second[h, d].start()
            out_ref[rows[h], rows_at(me, LANES)] = result

    fill(1)
    for d in range(7):
        source = lax.rem(me + 7 - d, 8)

        @pl.when(source < CHUNKS)
        def _(d=d):
            for h in range(2):
                second[h, d].wait_recv()

    for d, peer in enumerate(peers):

        @pl.when(peer < CHUNKS)
        def _(d=d):
            for h in range(2):
                first[h, d].wait_send()

    @pl.when(me < CHUNKS)
    def _():
        for copy in second.values():
            copy.wait_send()


def nothing():
    pass


def column():
    line = lax.axis_index("cin")
    base, y = line // 4 * 4, lax.rem(line, 4)
    return [base + lax.rem(y + d, 4) for d in range(1, 4)], lax.rem(line + 4, 8)


def all_outer():
    me, core = lax.axis_index("cout"), lax.axis_index("section")
    out = [{"section": 1 - core, "cout": me}]
    for peer in others("cout"):
        out.append({"section": core, "cout": peer})
        out.append({"section": 1 - core, "cout": peer})
    return out


def joined_phase(
    act_ref, parity_ref, weight_ref, input_ref, place_ref, place_load, back_ref, joined_ref, pre_ref, backsum_ref,
    moved_ref, part, sbuf, rbuf, own, pbuf, bsend, brecv, tsend, trecv, send, recv, send2, recv2, psem, qsem, send3,
    recv3,
):
    me, core = lax.axis_index("cout"), lax.axis_index("section")
    line = lax.axis_index("cin")
    rows = input_ref.shape[0]
    peers = others("cout")
    column_peers, across = column()
    pair = remote(back_ref.at[1 - core], pbuf, psem, qsem, {"section": 1 - core, "cout": me})
    pair.start()
    first = {}
    for h, (at, size) in enumerate(HALVES):
        span = slice(at, at + size)
        moved_ref[:, span] = dot(act_ref[...], parity_ref[:, span], NN, BF)
        part[:, span] = dot(weight_ref[...], moved_ref[:, span], TN)
        for d, peer in enumerate(peers):
            sbuf[d, :, span] = part[rows_at(peer, rows), span].astype(BF)
            first[h, d] = remote(
                sbuf.at[d, :, span], rbuf.at[d, :, span], send.at[7 * h + d], recv.at[7 * h + d], {"cout": peer}
            )
            first[h, d].start()
    pair.wait_recv()

    def both(at):
        return back_ref[core, at, :].astype(F32) + pbuf[at, :].astype(F32)

    y, z = lax.rem(line, 4), line // 4
    third = []
    for d, peer in enumerate(column_peers):
        for q in range(2):
            bsend[d, q] = both(rows_at(q * 4 + lax.rem(peer, 4), rows)).astype(BF)
        copy = remote(bsend.at[d], brecv.at[d], send3.at[d], recv3.at[d], {"cin": peer})
        copy.start()
        third.append(copy)
    place_load.wait()
    pre_ref[...] = dot(input_ref[...], place_ref[...], NN) + part[rows_at(me, rows), :]
    target, place = me // 4, lax.rem(me, 4)
    slot = core * 4 + place
    second = {}
    for h, (at, size) in enumerate(HALVES):
        span = slice(at, at + size)
        total = pre_ref[:, span]
        for d in range(7):
            first[h, d].wait_recv()
            total = total + rbuf[d, :, span].astype(F32)
        pre_ref[:, span] = total
        own[:, span] = gate(total).astype(BF)
        lanes = pl.ds(pl.multiple_of(core * PIX + at, LANES), size)
        for d in range(8):
            copy = remote(
                own.at[:, span],
                joined_ref.at[rows_at(place, rows), lanes],
                send2.at[8 * h + d],
                recv2.at[8 * h + slot],
                {"section": target, "cout": lax.rem(me + d, 8)},
            )
            second[h, d] = copy
            if d:
                copy.start()
            else:

                @pl.when(target != core)
                def _(copy=copy):
                    copy.start()

                @pl.when(target == core)
                def _(span=span, lanes=lanes):
                    joined_ref[rows_at(place, rows), lanes] = own[:, span]

    for d in range(3):
        third[d].wait_recv()

    def column_sum(q):
        value = both(rows_at(q * 4 + y, rows))
        for d in range(3):
            value = value + brecv[d, q].astype(F32)
        return value

    tsend[...] = column_sum(1 - z).astype(BF)
    third.append(remote(tsend, trecv, send3.at[3], recv3.at[3], {"cin": across}))
    third[3].start()
    backsum_ref[...] = column_sum(z)
    for h, (at, size) in enumerate(HALVES):
        for image in range(2):
            for k in range(4):
                mine = (core == image) & (me == core * 4 + k)
                arrival = remote(
                    own.at[:, at : at + size],
                    joined_ref.at[k * rows : (k + 1) * rows, image * PIX + at : image * PIX + at + size],
                    send2.at[0],
                    recv2.at[8 * h + image * 4 + k],
                    {"section": core, "cout": me},
                )

                @pl.when(jnp.logical_not(mine))
                def _(arrival=arrival):
                    arrival.wait_recv()

    third[3].wait_recv()
    backsum_ref[...] = backsum_ref[...] + trecv[...].astype(F32)
    pair.wait_send()
    for copy in third:
        copy.wait_send()
    for h in range(2):
        for d in range(7):
            first[h, d].wait_send()
            second[h, d + 1].wait_send()

        @pl.when(target != core)
        def _(h=h):
            second[h, 0].wait_send()


def front_body(
    feature_ref, grads_ref, natural_ref, spot_ref, kernel_far, spread_far, stride_far, parity_far, weight_ref, input_ref,
    place_far, patches_far, hidden_ref, placed_far, joined_ref, pre_ref, backsum_ref, moved_ref,
    own, grads_own, gathered, grads_gathered, grid, wide, kernel_ref, patches_ref, part_ref, grad_ref, spread_ref, stride_ref, placed_ref, back_ref,
    total_ref, parity_ref, place_ref, act_ref, local, gsend, grecv, isbuf, irbuf, isend, irecv, isend2, irecv2, *joins,
):
    met = signal(all_outer() + [{"cin": p} for p in others("cin")])
    loads = [
        started(far, near, local.at[n])
        for n, (far, near) in enumerate(
            (
                (kernel_far, kernel_ref),
                (spread_far, spread_ref),
                (stride_far, stride_ref),
                (parity_far, parity_ref),
                (place_far, place_ref),
            )
        )
    ]
    saves = [
        pltpu.make_async_copy(patches_ref, patches_far, local.at[5]),
        pltpu.make_async_copy(placed_ref, placed_far, local.at[6]),
    ]
    cotangent = gather_phase(
        met, feature_ref, grads_ref, natural_ref, spot_ref, patches_ref, saves[0], grad_ref, own, grads_own, gathered,
        grads_gathered, grid, wide, gsend, grecv,
    )
    loads[0].wait()

    @pl.when(lax.axis_index("cin") == CHUNKS)
    def _():
        hidden_ref[...] = jnp.zeros_like(hidden_ref)

    def fill(stage):
        if stage == 0:
            cotangent()
            total_ref[...] = jnp.zeros_like(total_ref)
            loads[1].wait()
            loads[2].wait()
        for plane, tap, at in TAPS[:5] if stage == 0 else TAPS[5:]:
            start, size = RANGES[plane]
            for image in range(2):
                placed_ref[:, 2 * at + image * size : 2 * at + (image + 1) * size] = dot(
                    grad_ref[image], spread_ref[:, at : at + size], NN, BF
                )
            term = dot(stride_ref[tap], placed_ref[:, 2 * at : 2 * (at + size)], TN)
            for image in range(2):
                total_ref[image, :, start : start + size] += term[:, image * size : (image + 1) * size]
        if stage == 1:
            saves[1].start()
            back_ref[...] = total_ref[...].astype(BF)

    def prepare(rows):
        part_ref[rows] = dot(kernel_ref[:, rows], patches_ref[...], TN)

    def finish(total, rows):
        hidden_ref[rows] = total
        return gate(total).astype(BF)

    inner_exchange(
        nothing,
        prepare,
        lambda j, rows: part_ref[rows, rows_at(j, LANES)],
        finish,
        fill,
        act_ref,
        isbuf,
        irbuf,
        (isend, irecv, isend2, irecv2),
    )
    loads[3].wait()
    joined_phase(
        act_ref, parity_ref, weight_ref, input_ref, place_ref, loads[4], back_ref, joined_ref, pre_ref, backsum_ref,
        moved_ref, *joins,
    )
    for save in saves:
        save.wait()


def second_phase(
    met, weight_ref, joined_ref, back_ref, masked_ref, act_ref, pair, pbuf, mine, sbuf, rbuf, psem, qsem, send, recv,
    send2, recv2, rsend, rrecv,
):
    me, core = lax.axis_index("cin"), lax.axis_index("section")
    sibling = {"section": 1 - core, "cin": me}
    rows = back_ref.shape[0]
    peers = others("cin")
    swaps = []
    for h, (at, size) in enumerate(HALVES):
        span = slice(at, at + size)
        lanes = pl.ds(pl.multiple_of((1 - core) * PIX + at, LANES), size)
        pair[:, span] = dot(weight_ref[...], joined_ref[:, lanes], TN, BF)
        if h == 0:
            met()
        copy = remote(pair.at[:, span], pbuf.at[:, span], psem.at[h], qsem.at[h], sibling)
        copy.start()
        swaps.append(copy)
    first, second = {}, {}
    own = rows_at(me, rows)
    for h, (at, size) in enumerate(HALVES):
        span = slice(at, at + size)
        lanes = pl.ds(pl.multiple_of(core * PIX + at, LANES), size)
        mine[:, span] = dot(weight_ref[...], joined_ref[:, lanes], TN)
        swaps[h].wait_recv()
        for d, peer in enumerate(peers):
            block = rows_at(peer, rows)
            sbuf[d, :, span] = (mine[block, span] + pbuf[block, span].astype(F32)).astype(BF)
            first[h, d] = remote(
                sbuf.at[d, :, span], rbuf.at[d, :, span], send.at[7 * h + d], recv.at[7 * h + d], {"cin": peer}
            )
            first[h, d].start()
    relays = {}
    for h, (at, size) in enumerate(HALVES):
        span = slice(at, at + size)
        lanes = pl.ds(pl.multiple_of(core * PIX + at, LANES), size)
        hidden = mine[own, span] + pbuf[own, span].astype(F32)
        for d in range(7):
            first[h, d].wait_recv()
            hidden = hidden + rbuf[d, :, span].astype(F32)
        masked_ref[own, lanes] = (back_ref[:, span] * slope(hidden)).astype(BF)
        spot = masked_ref.at[own, lanes]
        for d, peer in enumerate(peers):
            second[h, d] = remote(spot, spot, send2.at[7 * h + d], recv2.at[7 * h + d], {"cin": peer})
            second[h, d].start()
        relays[h, 7] = remote(spot, spot, rsend.at[8 * h + 7], rrecv.at[8 * h + 7], sibling)
        relays[h, 7].start()
        act_ref[:, span] = gate(hidden).astype(BF)
    for h, (at, size) in enumerate(HALVES):
        lanes = pl.ds(pl.multiple_of(core * PIX + at, LANES), size)
        for d in range(7):
            spot = masked_ref.at[rows_at(lax.rem(me + 7 - d, 8), rows), lanes]
            second[h, d].wait_recv()
            relays[h, d] = remote(spot, spot, rsend.at[8 * h + d], rrecv.at[8 * h + d], sibling)
            relays[h, d].start()
    for copy in relays.values():
        copy.wait_recv()
    for copy in swaps + list(first.values()) + list(second.values()) + list(relays.values()):
        copy.wait_send()


def input_phase(
    weight_ref, masked_ref, pre_ref, act_ref, joined_ref, place_ref, place_load, out_ref, second_ref, reduce_ref,
    reduce_save, input_ref, sbuf, rbuf, own, send, recv, send2, recv2, send3, recv3, rsend, rrecv,
):
    me, core = lax.axis_index("cout"), lax.axis_index("section")
    line = lax.axis_index("cin")
    rows = pre_ref.shape[0]
    peers = others("cout")
    column_peers, across = column()
    first = []
    for h, (at, size) in enumerate(HALVES):
        span = slice(at, at + size)
        for k in range(4):
            for image in range(2):
                n = k * 2 + image
                mine = (core == image) & (me == core * 4 + k)
                sbuf[n, :, span] = dot(
                    weight_ref[k * rows : (k + 1) * rows, :],
                    masked_ref[:, image * PIX + at : image * PIX + at + size],
                    NN,
                    BF,
                )
                copy = remote(
                    sbuf.at[n, :, span],
                    rbuf.at[me, :, span],
                    send.at[8 * h + n],
                    recv.at[8 * h + me],
                    {"section": image, "cout": core * 4 + k},
                )
                first.append((mine, copy))

                @pl.when(jnp.logical_not(mine))
                def _(copy=copy):
                    copy.start()

                @pl.when(mine)
                def _(n=n, span=span):
                    rbuf[me, :, span] = sbuf[n, :, span]

    def block(source):
        return second_ref.at[rows_at(source, rows), rows_at(core, PIX)]

    def handed(slot, source, src):
        copy = remote(src, block(source), rsend.at[slot], rrecv.at[slot], {"section": 1 - core, "cin": line})
        copy.start()
        return copy

    second_ref[rows_at(line, rows), rows_at(core, PIX)] = act_ref[...]
    third = []
    for d, peer in enumerate(column_peers + [across]):
        copy = remote(act_ref, block(line), send3.at[d], recv3.at[d], {"cin": peer})
        copy.start()
        third.append(copy)
    relays = [handed(7, line, act_ref)]
    reduce_ref[...] = dot(joined_ref[...], masked_ref[...], NT)
    reduce_save.start()
    third[3].wait_recv()
    for d, peer in enumerate(column_peers):
        copy = remote(block(across), block(across), send3.at[4 + d], recv3.at[4 + d], {"cin": peer})
        copy.start()
        third.append(copy)
    relays.append(handed(3, across, block(across)))
    second = []
    for h, (at, size) in enumerate(HALVES):
        span = slice(at, at + size)
        total = jnp.zeros((rows, size), F32)
        for k in range(8):
            arrival = remote(
                sbuf.at[0, :, span],
                rbuf.at[k, :, span],
                send.at[0],
                recv.at[8 * h + k],
                {"section": core, "cout": me},
            )

            @pl.when(jnp.logical_not((me == k) & (me // 4 == core)))
            def _(arrival=arrival):
                arrival.wait_recv()

            total = total + rbuf[k, :, span].astype(F32)
        own[:, span] = (total * slope(pre_ref[:, span])).astype(BF)
        for d, peer in enumerate(peers):
            copy = remote(
                own.at[:, span],
                out_ref.at[rows_at(me, rows), span],
                send2.at[7 * h + d],
                recv2.at[7 * h + d],
                {"cout": peer},
            )
            copy.start()
            second.append(copy)
    out_ref[rows_at(me, rows), :] = own[...]
    place_load.wait()
    input_ref[...] = dot(own[...], place_ref[...], NT, BF)
    base, y = line // 4 * 4, lax.rem(line, 4)
    for d in (0, 1, 2, 4, 5, 6):
        turn = lax.rem(y + 3 - d % 4, 4)
        source = base + turn if d < 3 else 4 - base + turn
        third[d].wait_recv()
        relays.append(handed(d, source, block(source)))
    for copy in second:
        copy.wait_recv()

    def settle():
        for copy in relays:
            copy.wait_recv()
        reduce_save.wait()
        for copy in second + relays + third:
            copy.wait_send()
        for mine, copy in first:

            @pl.when(jnp.logical_not(mine))
            def _(copy=copy):
                copy.wait_send()

    return settle


def last_phase(
    masked_ref, kernel_ref, kernel_load, patches_ref, patches_load, expand_ref, place_ref, place_load, inner_ref,
    local_far, fbuf, ebuf, total_ref, wide, local, near, sbuf, rbuf, send, recv, wsend, wrecv,
):
    me, core = lax.axis_index("cout"), lax.axis_index("section")
    rows = sbuf.shape[1]
    size = masked_ref.shape[0]
    peers = others("cout")
    sibling = {"section": 1 - core, "cout": me}
    swaps = [remote(expand_ref, ebuf, wsend.at[9], wrecv.at[9], sibling)]
    swaps[0].start()
    lane = lax.broadcasted_iota(jnp.int32, (1, PIX), 1)
    kernel_load.wait()
    copies = [
        remote(sbuf.at[peer], rbuf.at[d], send.at[d], recv.at[d], {"cout": peer}) for d, peer in enumerate(peers)
    ]
    for h in range(2):
        span = slice(h * size // 2, (h + 1) * size // 2)
        for tx in range(3):
            for ty in (1, 0, 2):
                dy = ty - 1
                term = dot(kernel_ref[3 * ty + tx, span, :], masked_ref[...], NN)
                if dy:
                    keep = (lane - 32 * dy >= 0) & (lane - 32 * dy < PIX)
                    wide[...] += jnp.where(keep, pltpu.roll(term, (PIX + 32 * dy) % PIX, 1), 0.0)
                else:
                    wide[...] = term
            if tx == 0:
                total_ref[...] = pltpu.roll(wide[...], PIX - 1, 1)
            elif tx == 1:
                total_ref[...] += wide[...]
            else:
                total_ref[...] += pltpu.roll(wide[...], 1, 1)
        for j in range(4):
            sbuf[4 * h + j] = total_ref[j * rows : (j + 1) * rows, :].astype(BF)
        for d, peer in enumerate(peers):

            @pl.when(peer // 4 == h)
            def _(d=d):
                copies[d].start()

    patches_load.wait()
    for t in range(9):
        local[t] = dot(patches_ref[t * size : (t + 1) * size, :], masked_ref[...], NT, BF)
        copy = remote(local.at[t], fbuf.at[t], wsend.at[t], wrecv.at[t], sibling)
        copy.start()
        swaps += [copy, started(local.at[t], local_far.at[t], near.at[t])]
    total = sbuf[me].astype(F32)
    for d in range(7):
        copies[d].wait_recv()
        total = total + rbuf[d].astype(F32)
    high = total.astype(BF)
    rest = total - high.astype(F32)
    middle = rest.astype(BF)
    low = (rest - middle.astype(F32)).astype(BF)
    place_load.wait()
    inner_ref[...] = (
        dot(low, place_ref[...], NT) + dot(middle, place_ref[...], NT) + dot(high, place_ref[...], NT)
    )
    for copy in swaps:
        copy.wait()
    for copy in copies:
        copy.wait_send()


def rear_body(
    reduce_weight_ref, joined_ref, back_ref, pre_ref, place_parity_far, weight_ref, parity_ref, hidden_ref, act_far,
    placed_far, kernel_far, patches_far, place_far,
    reduce_far, own_input_ref, expand_far, stride_far, inner_ref, local_far, fbuf, ebuf,
    second_masked, second_own, place_parity_ref, reduce_ref, input_ref, second_ref, act_ref, placed_ref, kernel_ref,
    patches_ref, place_ref, expand_ref, stride_ref, part, masked_ref, local,
    pair, pbuf, mine, ssbuf, srbuf, psem, qsem, ssend, srecv, ssend2, srecv2, srsend, srrecv,
    jsbuf, jrbuf, jown, jsend, jrecv, jsend2, jrecv2, jsend3, jrecv3, jrsend, jrrecv,
    isbuf, irbuf, isend, irecv, isend2, irecv2, *lasts,
):
    met = signal(all_outer() + [{"cin": p} for p in others("cin")])
    loads = [
        started(far, near, local.at[9 + n])
        for n, (far, near) in enumerate(
            (
                (act_far, act_ref),
                (place_parity_far, place_parity_ref),
                (placed_far, placed_ref),
                (kernel_far, kernel_ref),
                (patches_far, patches_ref),
                (place_far, place_ref),
            )
        )
    ]
    second_phase(
        met, reduce_weight_ref, joined_ref, back_ref, second_masked, second_own, pair, pbuf, mine, ssbuf, srbuf, psem,
        qsem, ssend, srecv, ssend2, srecv2, srsend, srrecv,
    )
    settle = input_phase(
        reduce_weight_ref, second_masked, pre_ref, second_own, joined_ref, place_parity_ref, loads[1], input_ref,
        second_ref, reduce_ref, pltpu.make_async_copy(reduce_ref, reduce_far, local.at[16]), own_input_ref, jsbuf, jrbuf,
        jown, jsend, jrecv, jsend2, jrecv2, jsend3, jrecv3, jrsend, jrrecv,
    )
    saves = []

    def prepare(rows):
        part[rows] = dot(weight_ref[rows], input_ref[...], NN, BF)

    def fill(stage):
        if stage == 0:
            loads[0].wait()
            loads[2].wait()
            expand_ref[...] = dot(act_ref[...], input_ref[...], NT, BF)
            saves.append(started(expand_ref, expand_far, local.at[15]))
            settle()
        for plane, tap, at in TAPS[:4] if stage == 0 else TAPS[4:]:
            start, size = RANGES[plane]
            stride_ref[tap] = (
                dot(placed_ref[:, 2 * at : 2 * at + size], second_ref[:, start : start + size], NT)
                + dot(
                    placed_ref[:, 2 * at + size : 2 * (at + size)],
                    second_ref[:, PIX + start : PIX + start + size],
                    NT,
                )
            ).astype(BF)
            saves.append(started(stride_ref.at[tap], stride_far.at[tap], local.at[tap]))

    def finish(total, rows):
        return (total * slope(hidden_ref[rows])).astype(BF)

    inner_exchange(
        nothing,
        prepare,
        lambda j, rows: dot(part[rows], parity_ref[rows_at(j, LANES), :], NT),
        finish,
        fill,
        masked_ref,
        isbuf,
        irbuf,
        (isend, irecv, isend2, irecv2),
    )
    last_phase(
        masked_ref, kernel_ref, loads[3], patches_ref, loads[4], expand_ref, place_ref, loads[5], inner_ref, local_far,
        fbuf, ebuf, *lasts,
    )
    for save in saves:
        save.wait()


def tail_body(
    stride_ref, first_ref, other_ref, expand_ref, expand_other_ref, reduce_ref, inner_ref, input_ref,
    stride_out, first_out, expand_out, reduce_out, inner_out, input_out,
):
    @pl.when(pl.program_id(0) == 0)
    def _():
        inner_out[...] = inner_ref[...]
        input_out[...] = input_ref[...]
        reduce_out[...] = reduce_ref[...]
        expand_out[...] = expand_ref[...].astype(F32) + expand_other_ref[...].astype(F32)

    stride_out[...] = stride_ref[...].astype(F32)
    first_out[...] = first_ref[...].astype(F32) + other_ref[...].astype(F32)


def tail(stride, first, other, expand, expand_other, reduce, inner, own_input):
    steps = 3

    def tap(array):
        return pl.BlockSpec((array.shape[0] // steps,) + array.shape[1:], lambda t: (t, 0, 0))

    def whole(array):
        return pl.BlockSpec(array.shape, lambda t: (0, 0))

    return pl.pallas_call(
        tail_body,
        grid=(steps,),
        out_shape=(
            jax.ShapeDtypeStruct(stride.shape, F32),
            jax.ShapeDtypeStruct(first.shape, F32),
            jax.ShapeDtypeStruct(expand.shape, F32),
            jax.ShapeDtypeStruct(reduce.shape, F32),
            jax.ShapeDtypeStruct(inner.shape, F32),
            jax.ShapeDtypeStruct(own_input.shape, BF),
        ),
        in_specs=[tap(stride), tap(first), tap(other)]
        + [whole(expand), whole(expand_other), whole(reduce), whole(inner), whole(own_input)],
        out_specs=(tap(stride), tap(first), whole(expand), whole(reduce), whole(inner), whole(own_input)),
        compiler_params=pltpu.CompilerParams(vmem_limit_bytes=56 * 2**20),
    )(stride, first, other, expand, expand_other, reduce, inner, own_input)


def dma(*shape):
    return pltpu.SemaphoreType.DMA(shape)


def vb(*shape):
    return pltpu.VMEM(shape, BF)


def vf(*shape):
    return pltpu.VMEM(shape, F32)


def shards(features, block, first_kernel, expand_weight, reduce_weight, stride_kernel, output_grad):
    channels = first_kernel.shape[1]
    narrow, wide = features.shape[2], block.shape[2]
    outer = stride_kernel.shape[1]
    put_natural = jnp.asarray(place_natural(), BF)
    put_parity = jnp.asarray(place_parity(), BF)
    to_parity = jnp.asarray(natural_to_parity(), BF)

    patches, first_hidden, placed, joined, joined_pre, back_second, act_parity = call(
        front_body,
        [
            ((9 * channels, PIX), BF),
            ((channels, LANES), F32),
            ((channels, 2 * PLACED), BF),
            ((channels, 2 * PIX), BF),
            ((wide, PIX), F32),
            ((wide, PIX), F32),
            ((channels, PIX), BF),
        ],
        [
            vb(TALL, PIX),
            vb(TALL, 512),
            vb(8 * TALL, PIX),
            vb(8 * TALL, 512),
            vf(channels, PIX),
            vf(channels, PIX),
            vb(9 * channels, channels),
            vb(9 * channels, PIX),
            vf(channels, PIX),
            vb(2, channels, 256),
            vb(256, PLACED),
            vb(9, channels, outer),
            vb(channels, 2 * PLACED),
            vb(2, outer, PIX),
            vf(2, outer, PIX),
            vb(PIX, PIX),
            vb(SIDE * SIDE, PIX),
            vb(channels, PIX),
            dma(7),
            dma(14),
            dma(14),
            vb(8, channels, LANES),
            vb(7, channels, LANES),
            dma(14),
            dma(14),
            dma(14),
            dma(14),
            vf(outer, PIX),
            vb(7, wide, PIX),
            vb(7, wide, PIX),
            vb(wide, PIX),
            vb(outer, PIX),
            vb(3, 2, wide, PIX),
            vb(3, 2, wide, PIX),
            vb(wide, PIX),
            vb(wide, PIX),
            dma(14),
            dma(14),
            dma(16),
            dma(16),
            pltpu.SemaphoreType.DMA,
            pltpu.SemaphoreType.DMA,
            dma(4),
            dma(4),
        ],
        0,
        features[0].T,
        output_grad.transpose(0, 2, 1),
        put_natural,
        jnp.asarray(place_grad(), BF),
        first_kernel.reshape(9 * channels, channels),
        jnp.asarray(spread_grad(), BF),
        stride_kernel.transpose(0, 2, 1),
        to_parity,
        expand_weight,
        block[0].T,
        put_parity,
        far_in=(4, 5, 6, 7, 10),
        far_out=(0, 2),
    )

    reduce_local, input_own, expand_local, stride_local, inner_own, first_local, first_other, expand_other = call(
        rear_body,
        [
            (reduce_weight.shape, F32),
            ((wide, SIDE * SIDE), BF),
            (expand_weight.shape, BF),
            ((9, channels, outer), BF),
            ((narrow, SIDE * SIDE), F32),
            ((9, channels, channels), BF),
            ((9, channels, channels), BF),
            (expand_weight.shape, BF),
        ],
        [
            vb(outer, 2 * PIX),
            vb(wide, PIX),
            vb(SIDE * SIDE, PIX),
            vf(*reduce_weight.shape),
            vb(outer, PIX),
            vb(outer, 2 * PIX),
            vb(channels, PIX),
            vb(channels, 2 * PLACED),
            vb(9, channels, channels),
            vb(9 * channels, PIX),
            vb(SIDE * SIDE, PIX),
            vb(*expand_weight.shape),
            vb(9, channels, outer),
            vb(channels, PIX),
            vb(channels, PIX),
            dma(17),
            vb(outer, PIX),
            vb(outer, PIX),
            vf(outer, PIX),
            vb(7, wide, PIX),
            vb(7, wide, PIX),
            dma(2),
            dma(2),
            dma(14),
            dma(14),
            dma(14),
            dma(14),
            dma(16),
            dma(16),
            vb(8, wide, PIX),
            vb(8, wide, PIX),
            vb(wide, PIX),
            dma(16),
            dma(16),
            dma(14),
            dma(14),
            dma(7),
            dma(7),
            dma(8),
            dma(8),
            vb(8, channels, LANES),
            vb(7, channels, LANES),
            dma(14),
            dma(14),
            dma(14),
            dma(14),
            vf(channels // 2, PIX),
            vf(channels // 2, PIX),
            vb(9, channels, channels),
            dma(9),
            vb(8, narrow, PIX),
            vb(7, narrow, PIX),
            dma(7),
            dma(7),
            dma(10),
            dma(10),
        ],
        1,
        reduce_weight,
        joined,
        back_second,
        joined_pre,
        put_parity,
        expand_weight,
        to_parity,
        first_hidden,
        act_parity,
        placed,
        first_kernel,
        patches,
        put_natural,
        far_in=(4, 8, 9, 10, 11, 12),
        far_out=(0, 2, 3, 5, 6, 7),
    )
    stride_gradient, first_gradient, expand_gradient, reduce_gradient, inner_own, input_own = tail(
        stride_local, first_local, first_other, expand_local, expand_other, reduce_local, inner_own, input_own
    )
    return (
        inner_own.T[None],
        input_own.T[None],
        first_gradient,
        expand_gradient,
        reduce_gradient,
        stride_gradient.transpose(0, 2, 1),
    )


def solution(mesh):
    return jax.shard_map(
        shards,
        mesh=mesh,
        in_specs=(
            P("section", None, ("cin", "cout")),
            P("section", None, ("cin", "cout")),
            P(None, "cin", "cout"),
            P("cout", "cin"),
            P(("cin", "section"), "cout"),
            P(None, "cout", ("section", "cin")),
            P(None, None, ("section", "cin", "cout")),
        ),
        out_specs=(
            P("section", None, ("cin", "cout")),
            P("section", None, ("cin", "cout")),
            P(None, "cin", "cout"),
            P("cout", "cin"),
            P(("cin", "section"), "cout"),
            P(None, "cout", ("section", "cin")),
        ),
        check_vma=False,
    )
```

time: 967 us -> 189 us (0.20)
  waiting for transfers between devices: 425 us -> 0 us
  local copies, waits for them, and re-layouts: 203 us -> 0 us
  blocking collectives: 203 us -> 0 us
  Pallas kernels: 0 us -> 187 us
  matrix products: 70.4 us -> 0 us
  other arithmetic: 39.2 us -> 0 us
  between operations: 15.9 us -> 0.65 us
    unnamed x12 -> x0, waiting for transfers between devices: 227 us -> none
    psum x2 -> x0, waiting for transfers between devices: 198 us -> none  [the longest x1 195 us: shards(): back_whole = lax.psum(back_part, ('section', 'cin'))]
    all_gather x6 -> x0, blocking collectives: 193 us -> none  [the longest x4 121 us: gather_outer(): return lax.all_gather(shard, 'cout', axis=2, tiled=True)]
    pallas_call x0 -> x3, Pallas kernels: none -> 187 us  [the longest x2 178 us: call(): pl.pallas_call(body, out_shape=tuple((jax.ShapeDtypeStruct(s, d) for s, d...]
    dot_general x51 -> x0, matrix products: 70.4 us -> none  [the longest x9 14.4 us: conv_half_weight(): lax.dot_general(window, flat, (((0,), (0,)), ((), ())), preferred_element...]
    slice x17 -> x0, local copies, waits for them, and re-layouts: 67.9 us -> none  [the longest x5 52.9 us: conv_half_back(): canvas[:, 1:side + 1, 1:side + 1, :]]
    reshape x31 -> x0, local copies, waits for them, and re-layouts: 51.5 us -> none  [the longest x8 17.2 us: conv_same_back(): padded[:, 2 - row:2 - row + side, 2 - column:2 - column + side, :]]
    unnamed x123 -> x0, local copies, waits for them, and re-layouts: 39.9 us -> none
  transfers between devices with their start and end apart: 7 -> 0, of which waited for: 6 -> 0; matrix products, arithmetic and copies ran while one was open for 20% -> 0% of each run, Pallas kernels for 0% -> 0%
where the time goes in v1:
time: 189 us; the launch traced here: 188 us
  Pallas kernels  187 us (99%)
    pallas_call x2, Pallas kernels, call(): pl.pallas_call(body, out_shape=tuple((jax.ShapeDtypeStruct(s, d) for s, d...  178 us
    pallas_call x1, Pallas kernels, tail(): pl.pallas_call(tail_body, grid=(steps,), out_shape=(jax.ShapeDtypeStruct(...  9.57 us

profile of v1, /device:TPU:0, one launch (start us, length us, event | category | flops | bytes accessed | tf_op | source)
XLA Modules:
  0.0 188.1 jit_solution(4415789162297826615)
XLA Ops:
  0.6 71.4 %shard_map.163 = (bf16[2880,896]{1,0:T(8,128)(2,1)}, f32[320,128]{1,0:T(8,128)}, bf16[320,5632]{1,0:T(8,128)(2,1)}, bf16[320,1792]{1,0:T(8,128)(2,1)}, f32[80,89...) custom-call(bf16[40,784]{1,0:T(8,128)(2,1)} %bitcast.19, bf16[2,40,196]{2,1,0:T(8,128)(2,1)} %bitcast.20, ...), custom_call_target="tpu_custom_call" | custom-call | tf_op jit(solution)/shard_map/pallas_call | solution.py:135
  72.0 106.5 %shard_map.164 = (f32[320,640]{1,0:T(8,128)}, bf16[80,784]{1,0:T(8,128)(2,1)}, bf16[320,640]{1,0:T(8,128)(2,1)}, bf16[9,320,640]{2,1,0:T(8,128)(2,1)}, f32[40,78...) custom-call(bf16[320,640]{1,0:T(8,128)(2,1)} %reduce_weight_ref.1, ...), custom_call_target="tpu_custom_call" | custom-call | tf_op jit(solution)/shard_map/pallas_call | solution.py:135
  178.5 9.6 %shard_map.165 = (f32[9,320,640]{2,1,0:T(8,128)}, f32[9,320,320]{2,1,0:T(8,128)}, f32[320,640]{1,0:T(8,128)}, f32[320,640]{1,0:T(8,128)}, f32[40,784]{1,0:T(8,128)}, /*index=5*/bf16[80,784]{1,0:T(8,128)(2,1)}) custom-call(bf16[9,320,640]{2,1,0:T(8,128)(2,1)} %get-tuple-element.34.stride_ref, bf16[9,320,320]{2,1,0:T(8,128)(2,1)} %get-tuple-element.35.first_ref, ...), custom_call_target="tpu_custom_call" | custom-call | tf_op jit(solution)/shard_map/pallas_call | solution.py:839
